TPU v7x, 32 devices: a whole 2x2x4 slice. The times are simulated.
32 devices in a mesh: row: 8 (over z, y), col: 4 (over x, core).
Axes of the slice: x: 2, y: 2, z: 4, core: 2. Of those that a mesh axis runs over, the one named last changes fastest.
Arguments:
- hidden_in: bfloat16 [16384, 1024], P(('row', 'col')), may hold values from -6 to 6
- teacher: float32 [16384, 1024], P(('row', 'col')), may hold values from -6 to 6
- valid_mask: int32 [16384], replicated, may hold values from 0 to 1, as said below
- first_gain: float32 [1024], replicated, may hold values from 0.1 to 1.9
- second_gain: float32 [1024], replicated, may hold values from 0.1 to 1.9
- attention_in: bfloat16 [3, 1024, 1024], P(None, 'col', 'row'), may hold values from -0.1875 to 0.1875
- attention_out: bfloat16 [1024, 1024], P('row', 'col'), may hold values from -6 to 6
- feed_in: bfloat16 [2, 2624, 1024], P(None, 'col', 'row'), may hold values from -0.1875 to 0.1875
- feed_out: bfloat16 [1024, 2624], P('row', 'col'), may hold values from -0.125 to 0.125
Outputs:
- layer_out: bfloat16 [16384, 1024], P(('row', 'col'))
- loss: float32 [], replicated
- grad_input: float32 [16384, 1024], P(('row', 'col'))
- grad_first_gain: float32 [1024], replicated
- grad_second_gain: float32 [1024], replicated
- grad_attention_in: float32 [3, 1024, 1024], P(None, 'col', 'row')
- grad_attention_out: float32 [1024, 1024], P('row', 'col')
- grad_feed_in: float32 [2, 2624, 1024], P(None, 'col', 'row')
- grad_feed_out: float32 [1024, 2624], P('row', 'col')
Inputs may be any that keep to these rules, and one draw needn't show every extreme that they name: `valid_mask`: 1 marks a token that serves as a key and counts in the loss; the first token of every sequence of 2048 is 1.
All inputs are finite; a program needn't handle non-finite values.
Results may differ from a plain program's by a relative error of at most 0.012.
Values may be sent and summed in bfloat16 or wider, within the bound.
No kernel may reach another device: no remote copies, remote signals or barrier semaphores. Data moves between devices by JAX's collectives and lax.ppermute only.
A program may use at most 256 MiB of HBM per device.

v0:
```python
import jax
import jax.numpy as jnp
from jax import lax
from jax.sharding import PartitionSpec as P

D = 1024
HD = 64
SEQ_LEN = 2048
EPSILON = 1e-05
ROPE_BASE = 160000.0
FLOOR_SCORE = -1e30


def layer_norm(values, gain):
    center = values - jnp.mean(values, axis=1, keepdims=True)
    inverse = lax.rsqrt(jnp.mean(center * center, axis=1, keepdims=True) + EPSILON)
    normed = center * inverse
    return (normed, inverse, (normed * gain).astype(jnp.bfloat16))


def norm_back(grad_low, normed, inverse, gain):
    scaled = grad_low * gain
    inner = jnp.mean(scaled * normed, axis=1, keepdims=True)
    centered = scaled - jnp.mean(scaled, axis=1, keepdims=True)
    return (inverse * (centered - normed * inner), jnp.sum(grad_low * normed, axis=0))


def rotary_tables(rows, width):
    half = width // 2
    frequency = ROPE_BASE ** (-(jnp.arange(half, dtype=jnp.float32) * 2.0) / width)
    place = (jnp.arange(rows, dtype=jnp.int32) % SEQ_LEN).astype(jnp.float32)
    angle = place[:, None] * frequency[None, :]
    angle = jnp.concatenate([angle, angle], axis=1)
    return (jnp.cos(angle), jnp.sin(angle))


def rotate(values, cosine, sine):
    half = values.shape[-1] // 2
    turned = jnp.concatenate([-values[..., half:], values[..., :half]], axis=-1)
    return values * cosine[:, None, :] + turned * sine[:, None, :]


def rotate_back(grads, cosine, sine):
    half = grads.shape[-1] // 2
    moved = grads * sine[:, None, :]
    turned = jnp.concatenate([moved[..., half:], -moved[..., :half]], axis=-1)
    return grads * cosine[:, None, :] + turned


def block_scores(query, keys, live, start, block):
    base = start // SEQ_LEN * SEQ_LEN
    picked = lax.dynamic_slice_in_dim(query, start, block, 0)
    window = lax.dynamic_slice_in_dim(keys, base, SEQ_LEN, 0)
    allowed = lax.dynamic_slice_in_dim(live, base, SEQ_LEN, 0)
    scores = jnp.einsum(
        "qhd,khd->hqk", picked, window, preferred_element_type=jnp.float32
    ) * query.shape[2] ** (-0.5)
    return (jnp.where(allowed[None, None, :] > 0, scores, FLOOR_SCORE), picked, window, base)


def attend(query, keys, values, live):
    rows, heads, width = query.shape
    block = min(512, SEQ_LEN)

    def one_block(index):
        start = index * block
        scores, picked, window, base = block_scores(query, keys, live, start, block)
        seq_values = lax.dynamic_slice_in_dim(values, base, SEQ_LEN, 0)
        top = jnp.max(scores, axis=2, keepdims=True)
        weights = jnp.exp(scores - top)
        total = jnp.sum(weights, axis=2, keepdims=True)
        probs = (weights / total).astype(jnp.bfloat16)
        mixed = jnp.einsum("hqk,khd->qhd", probs, seq_values, preferred_element_type=jnp.float32)
        return (mixed.astype(jnp.bfloat16), (top + jnp.log(total))[:, :, 0])

    mixed, log_total = lax.map(one_block, jnp.arange(rows // block, dtype=jnp.int32))
    return (mixed.reshape(rows, heads * width), log_total)


def attend_back(query, keys, values, live, log_total, grad_mixed):
    rows, heads, width = query.shape
    block = min(512, SEQ_LEN)
    scale = width ** (-0.5)
    zeros = jnp.zeros((rows, heads, width), jnp.float32)

    def one_block(index, carry):
        grad_query, grad_keys, grad_values = carry
        start = index * block
        scores, picked, window, base = block_scores(query, keys, live, start, block)
        probs = jnp.exp(scores - log_total[index][:, :, None])
        seq_values = lax.dynamic_slice_in_dim(values, base, SEQ_LEN, 0)
        grad_block = lax.dynamic_slice_in_dim(grad_mixed, start, block, 0)
        grad_probs = jnp.einsum(
            "qhd,khd->hqk", grad_block, seq_values, preferred_element_type=jnp.float32
        )
        inner = jnp.sum(probs * grad_probs, axis=2, keepdims=True)
        grad_scores = (probs * (grad_probs - inner)).astype(jnp.bfloat16)
        part_query = (
            jnp.einsum("hqk,khd->qhd", grad_scores, window, preferred_element_type=jnp.float32)
            * scale
        )
        part_keys = (
            jnp.einsum("hqk,qhd->khd", grad_scores, picked, preferred_element_type=jnp.float32)
            * scale
        )
        part_values = jnp.einsum(
            "hqk,qhd->khd",
            probs.astype(jnp.bfloat16),
            grad_block,
            preferred_element_type=jnp.float32,
        )
        grad_query = lax.dynamic_update_slice_in_dim(grad_query, part_query, start, 0)
        grad_keys = lax.dynamic_update_slice_in_dim(
            grad_keys, lax.dynamic_slice_in_dim(grad_keys, base, SEQ_LEN, 0) + part_keys, base, 0
        )
        grad_values = lax.dynamic_update_slice_in_dim(
            grad_values,
            lax.dynamic_slice_in_dim(grad_values, base, SEQ_LEN, 0) + part_values,
            base,
            0,
        )
        return (grad_query, grad_keys, grad_values)

    return lax.fori_loop(0, rows // block, one_block, (zeros, zeros, zeros))


def shards(
    hidden_in,
    teacher,
    valid_mask,
    first_gain,
    second_gain,
    attention_in,
    attention_out,
    feed_in,
    feed_out,
):
    columns = lax.axis_size("col")
    own_rows = hidden_in.shape[0]
    group = own_rows * columns
    own_start = lax.axis_index("col") * own_rows
    group_start = lax.axis_index("row") * group
    total_tokens = group * lax.axis_size("row")
    live_group = lax.dynamic_slice_in_dim(valid_mask, group_start, group, 0)
    live_own = lax.dynamic_slice_in_dim(live_group, own_start, own_rows, 0).astype(jnp.float32)
    valid_total = jnp.sum(valid_mask.astype(jnp.float32))
    joint_rows, attention_rows, feed_in_rows, feed_out_rows = (
        lax.all_gather(attention_in, "row", axis=2, tiled=True),
        lax.all_gather(attention_out, "row", axis=0, tiled=True),
        lax.all_gather(feed_in, "row", axis=2, tiled=True),
        lax.all_gather(feed_out, "row", axis=0, tiled=True),
    )
    inputs = hidden_in.astype(jnp.float32)
    normed_one, inverse_one, low_one = layer_norm(inputs, first_gain)
    joint = jnp.einsum(
        "rd,icd->ric",
        lax.all_gather(low_one, "col", axis=0, tiled=True),
        joint_rows,
        preferred_element_type=jnp.float32,
    )
    local_width = joint.shape[2]
    split = (group, local_width // HD, HD)
    cosine, sine = rotary_tables(group, HD)
    query = rotate(joint[:, 0].reshape(split), cosine, sine).astype(jnp.bfloat16)
    keys = rotate(joint[:, 1].reshape(split), cosine, sine).astype(jnp.bfloat16)
    values = joint[:, 2].reshape(split).astype(jnp.bfloat16)
    mixed, log_total = attend(query, keys, values, live_group)
    part = mixed
    branch = lax.psum_scatter(
        jnp.einsum("rc,oc->ro", part, attention_rows, preferred_element_type=jnp.float32),
        "col",
        scatter_dimension=0,
        tiled=True,
    )
    middle = inputs + branch
    normed_two, inverse_two, low_two = layer_norm(middle, second_gain)
    projected = jnp.einsum(
        "rd,ifd->rif",
        lax.all_gather(low_two, "col", axis=0, tiled=True),
        feed_in_rows,
        preferred_element_type=jnp.float32,
    )
    gate = projected[:, 0]
    upper = projected[:, 1]
    activated = (jax.nn.gelu(gate, approximate=False) * upper).astype(jnp.bfloat16)
    part = activated
    feed_branch = lax.psum_scatter(
        jnp.einsum("rf,of->ro", part, feed_out_rows, preferred_element_type=jnp.float32),
        "col",
        scatter_dimension=0,
        tiled=True,
    )
    result = middle + feed_branch
    error_term = result - teacher
    squares = jnp.sum(live_own * jnp.sum(error_term * error_term, axis=1))
    grad_result = (total_tokens * live_own)[:, None] * error_term / valid_total
    grad_low = grad_result.astype(jnp.bfloat16)
    piece = lax.all_gather(grad_low, "col", axis=0, tiled=True)
    part = activated
    grad_out = jnp.einsum("ro,rf->of", piece, part, preferred_element_type=jnp.float32)
    rows_grad = jnp.einsum("ro,of->rf", piece, feed_out_rows, preferred_element_type=jnp.float32)
    grad_act = rows_grad

    def geglu(first, second):
        return jax.nn.gelu(first, approximate=False) * second

    unused, pull = jax.vjp(geglu, gate, upper)
    grad_gate, grad_upper = pull(grad_act)
    grad_projected = jnp.stack([grad_gate, grad_upper], axis=1).astype(jnp.bfloat16)
    part = grad_projected
    grad_low_two = lax.psum_scatter(
        jnp.einsum("rif,ifd->rd", part, feed_in_rows, preferred_element_type=jnp.float32),
        "col",
        scatter_dimension=0,
        tiled=True,
    )
    grad_middle_norm, grad_second = norm_back(grad_low_two, normed_two, inverse_two, second_gain)
    grad_middle = grad_result + grad_middle_norm
    grad_branch = grad_middle.astype(jnp.bfloat16)
    piece = lax.all_gather(grad_branch, "col", axis=0, tiled=True)
    part = mixed
    grad_weight = jnp.einsum("ro,rc->oc", piece, part, preferred_element_type=jnp.float32)
    rows_grad = jnp.einsum("ro,oc->rc", piece, attention_rows, preferred_element_type=jnp.float32)
    grad_heads = rows_grad
    grad_attention_rows, grad_heads = (grad_weight, grad_heads)
    grad_mixed = grad_heads.astype(jnp.bfloat16)
    grad_query, grad_keys, grad_values = attend_back(
        query, keys, values, live_group, log_total, grad_mixed.reshape(split)
    )
    grad_joint = jnp.stack(
        [rotate_back(grad_query, cosine, sine), rotate_back(grad_keys, cosine, sine), grad_values],
        axis=1,
    )
    grad_joint = grad_joint.astype(jnp.bfloat16).reshape(group, 3, local_width)
    part = grad_joint
    grad_low_one = lax.psum_scatter(
        jnp.einsum("ric,icd->rd", part, joint_rows, preferred_element_type=jnp.float32).astype(
            jnp.bfloat16
        ),
        "col",
        scatter_dimension=0,
        tiled=True,
    ).astype(jnp.float32)
    grad_input_norm, grad_first = norm_back(grad_low_one, normed_one, inverse_one, first_gain)
    grad_input = grad_middle + grad_input_norm
    grad_joint_weight = jnp.einsum(
        "ric,rd->icd",
        grad_joint,
        lax.all_gather(low_one, "col", axis=0, tiled=True),
        preferred_element_type=jnp.float32,
    )
    grad_feed_weight = jnp.einsum(
        "rif,rd->ifd",
        grad_projected,
        lax.all_gather(low_two, "col", axis=0, tiled=True),
        preferred_element_type=jnp.float32,
    )
    grads = (
        lax.psum_scatter(
            grad_joint_weight.astype(jnp.bfloat16), "row", scatter_dimension=2, tiled=True
        ).astype(jnp.float32),
        lax.psum_scatter(
            grad_attention_rows.astype(jnp.bfloat16), "row", scatter_dimension=0, tiled=True
        ).astype(jnp.float32),
        lax.psum_scatter(
            grad_feed_weight.astype(jnp.bfloat16), "row", scatter_dimension=2, tiled=True
        ).astype(jnp.float32),
        lax.psum_scatter(
            grad_out.astype(jnp.bfloat16), "row", scatter_dimension=0, tiled=True
        ).astype(jnp.float32),
    )
    totals = lax.psum((grad_first, grad_second, squares), ("row", "col"))
    loss = totals[2] / (D * valid_total)
    return (
        result.astype(jnp.bfloat16),
        loss,
        grad_input,
        totals[0],
        totals[1],
        grads[0],
        grads[1],
        grads[2],
        grads[3],
    )


def solution(mesh):
    in_specs = (
        P(("row", "col"), None),
        P(("row", "col"), None),
        P(),
        P(),
        P(),
        P(None, "col", "row"),
        P("row", "col"),
        P(None, "col", "row"),
        P("row", "col"),
    )
    out_specs = (
        P(("row", "col"), None),
        P(),
        P(("row", "col"), None),
        P(),
        P(),
        P(None, "col", "row"),
        P("row", "col"),
        P(None, "col", "row"),
        P("row", "col"),
    )
    return jax.shard_map(shards, mesh=mesh, in_specs=in_specs, out_specs=out_specs, check_vma=False)
```

profile of v0, /device:TPU:0, one launch (start us, length us, event | category | flops | bytes accessed | tf_op | source)
XLA Modules:
  0.0 1042.4 jit_solution(1975161616662650184)
XLA Ops:
  13.8 36.6 %all_gather.28 = bf16[1024,256]{1,0:T(8,128)(2,1)} all-gather(bf16[128,256]{1,0:T(8,128)(2,1)S(1)} %copy-done.23), channel_id=1, replica_groups=mesh['row'=8,'col'=4] {'row'}, dimensions={0}, use_global_device_ids=true | all-gather | bytes 589824 | tf_op jit(solution)/shard_map/all_gather | solution.py:149
  60.2 35.2 %all-gather.8.cloned.1.call-done = bf16[2048,1024]{1,0:T(8,128)(2,1)} async-done(((bf16[512,1024]{1,0:T(8,128)(2,1)}), bf16[2048,1024]{1,0:T(8,128)(2,1)}) %all-gather.8.cloned.1.call-update) | async-done | bytes 4194320 | tf_op jit(solution)/shard_map/all_gather | solution.py:157
  104.2 52.4 %while.30 = (s32[]{:T(128)}, bf16[4,512,4,64]{1,3,2,0:T(8,128)(2,1)}, f32[4,4,512]{2,1,0:T(4,128)S(1)}, s32[2048]{0:T(1024)S(1)}, s32[4]{0:T(128)S(1)}, /*index=...) while((s32[]{:T(128)}, ...), condition=%wide.region_5.6_spmd, body=%wide.region_2.5_spmd.sunk | while | flops 1124204544 | bytes 53035200 | solution.py:76
  166.1 70.8 %reduce-scatter.15.cloned.1.call-done = f32[512,1024]{1,0:T(8,128)} async-done(((f32[2048,1024]{1,0:T(8,128)}), f32[512,1024]{1,0:T(8,128)}) %reduce-scatter.15.cloned.1.call-update) | async-done | bytes 2097168 | tf_op jit(solution)/shard_map/reduce_scatter | solution.py:169
  241.4 54.6 %all-gather.14.cloned.1.call-done = bf16[2,656,1024]{2,1,0:T(8,128)(2,1)} async-done(((bf16[2,656,128]{2,1,0:T(8,128)(2,1)}), bf16[2,656,1024]{2,1,0:T(8,128)(2,1)}) %all-gather.14.cloned.1.call-update) | async-done | bytes 2686992 | tf_op jit(solution)/shard_map/all_gather | solution.py:150
  296.0 34.6 %all-gather.12.cloned.1.call-done = bf16[2048,1024]{1,0:T(8,128)(2,1)} async-done(((bf16[512,1024]{1,0:T(8,128)(2,1)}), bf16[2048,1024]{1,0:T(8,128)(2,1)}) %all-gather.12.cloned.1.call-update) | async-done | bytes 4194320 | tf_op jit(solution)/shard_map/all_gather | solution.py:179
  330.6 8.5 fusion.59
  343.3 12.9 %multiply_convert_fusion.2 = (bf16[2048,656]{0,1:T(8,128)(2,1)}, f32[2048,656]{0,1:T(8,128)}) fusion(f32[2048,2,656]{0,2,1:T(8,128)S(1)} %fusion.59), kind=kLoop, calls=%fused_computation.63 | loop fusion | flops 88670208 | bytes 18808832 | tf_op jit(solution)/shard_map/convert_element_type | solution.py:185
  356.1 18.4 %all-gather.16.cloned.1.call-done = bf16[1024,656]{0,1:T(8,128)(2,1)} async-done(((bf16[128,656]{0,1:T(8,128)(2,1)}), bf16[1024,656]{0,1:T(8,128)(2,1)}) %all-gather.16.cloned.1.call-update) | async-done | bytes 1343504 | tf_op jit(solution)/shard_map/all_gather | solution.py:151
  374.5 8.9 fusion.111
  384.9 68.3 %reduce-scatter.17.cloned.1.call-done = f32[512,1024]{1,0:T(8,128)} async-done(((f32[2048,1024]{1,0:T(8,128)}), f32[512,1024]{1,0:T(8,128)}) %reduce-scatter.17.cloned.1.call-update) | async-done | bytes 2097168 | tf_op jit(solution)/shard_map/reduce_scatter | solution.py:187
  457.7 34.3 %all-gather.18.cloned.1.call-done = bf16[2048,1024]{1,0:T(8,128)(2,1)} async-done(((bf16[512,1024]{1,0:T(8,128)(2,1)}), bf16[2048,1024]{1,0:T(8,128)(2,1)}) %all-gather.18.cloned.1.call-update) | async-done | bytes 4194320 | tf_op jit(solution)/shard_map/all_gather | solution.py:198
  492.0 10.4 %fusion.66 = (bf16[2048,1,656]{0,2,1:T(8,128)(2,1)S(1)}, bf16[2048,1,656]{0,2,1:T(8,128)(2,1)S(1)}) fusion(f32[2048,656]{0,1:T(8,128)} %get-tuple-element.310, f32[2048,2,656]{0,2,1:T(8,128)} %copy-done.8, bf16[2048,1024]{1,0:T(8,128)(2,1)} %all-gather.18.cloned.1.call-done, bf16[1024,656]{0,1:T(8,128)(2,1)} %all-gather.16.cloned.1.call-done), kind=kOutput, calls=%fused_computation.92 | convolution fusion | flops 2775646208 | bytes 27033600 | tf_op jit(solution)/shard_map/ro,of->rf/dot_general | solution.py:201
  504.9 9.0 convolution_bitcast_fusion
  514.0 71.5 %reduce-scatter.19.cloned.1.call-done = f32[512,1024]{1,0:T(8,128)} async-done(((f32[2048,1024]{1,0:T(8,128)}), f32[512,1024]{1,0:T(8,128)}) %reduce-scatter.19.cloned.1.call-update) | async-done | bytes 2097168 | tf_op jit(solution)/shard_map/reduce_scatter | solution.py:211
  601.2 10.7 %fusion.74 = bf16[2,656,1024]{2,1,0:T(8,128)(2,1)} fusion(bf16[2048,1024]{1,0:T(8,128)(2,1)} %all-gather.12.cloned.1.call-done, bf16[2048,1,656]{0,2,1:T(8,128)(2,1)} %copy-done.33, bf16[2048,1,656]{0,2,1:T(8,128)(2,1)} %copy-done.32), kind=kOutput, calls=%fused_computation.103 | convolution fusion | flops 5506957312 | bytes 12255232 | tf_op jit(solution)/shard_map/rif,rd->ifd/dot_general | solution.py:252
  612.0 8.8 copy.35
  620.8 7.6 reshape.195
  635.0 167.3 %while.31 = (s32[]{:T(128)}, f32[2048,4,64]{0,2,1:T(8,128)}, f32[2048,4,64]{0,2,1:T(8,128)}, f32[2048,4,64]{0,2,1:T(8,128)}, s32[2048]{0:T(1024)S(1)}, /*index=5...) while((s32[]{:T(128)}, f32[2048,4,64]{0,2,1:T(8,128)}, ...), condition=%wide.region_19.20_spmd.clone, body=%wide.region_17.19_spmd.clone.sunk | while | flops 2750021632 | bytes 172564736 | solution.py:124
  644.1 9.4 multiply_reduce_fusion.8
  653.6 8.2 multiply_convert_fusion.5
  685.5 9.4 multiply_reduce_fusion.8
  694.9 8.2 multiply_convert_fusion.5
  727.6 9.4 multiply_reduce_fusion.8
  737.0 8.2 multiply_convert_fusion.5
  769.8 9.4 multiply_reduce_fusion.8
  779.2 8.1 multiply_convert_fusion.5
  835.4 7.4 bitcast_convert_fusion
  851.7 23.2 %reduce-scatter.23.cloned.1.call-done = bf16[128,256]{1,0:T(8,128)(2,1)} async-done(((bf16[1024,256]{1,0:T(8,128)(2,1)}), bf16[128,256]{1,0:T(8,128)(2,1)}) %reduce-scatter.23.cloned.1.call-update) | async-done | bytes 65552 | tf_op jit(solution)/shard_map/reduce_scatter | solution.py:262
  876.4 66.4 %reduce-scatter.25.cloned.1.call-done = bf16[128,768]{1,0:T(8,128)(2,1)} async-done(((bf16[1024,768]{1,0:T(8,128)(2,1)}), bf16[128,768]{1,0:T(8,128)(2,1)}) %reduce-scatter.25.cloned.1.call-update) | async-done | bytes 196624
  946.4 42.2 %reduce-scatter.21.cloned.1.call-done = bf16[512,1024]{1,0:T(8,128)(2,1)} async-done(((bf16[2048,1024]{1,0:T(8,128)(2,1)}), bf16[512,1024]{1,0:T(8,128)(2,1)}) %reduce-scatter.21.cloned.1.call-update) | async-done | bytes 1048592 | tf_op jit(solution)/shard_map/reduce_scatter | solution.py:236
  990.9 39.7 %all-reduce = (f32[]{:T(128)}, f32[1024]{0:T(1024)}, f32[1024]{0:T(1024)}) all-reduce(f32[]{:T(128)} %multiply_reduce_fusion.6, f32[1024]{0:T(1024)S(1)} %get-tuple-element.264, f32[1024]{0:T(1024)S(1)} %copy-done.30), channel_id=1, replica_groups=mesh['row'=8,'col'=4] {'row','col'}, use_global_device_ids=true, to_apply=%region_12.13 | all-reduce | flops 2049 | bytes 16392 | tf_op jit(solution)/shard_map/psum | solution.py:272
  (222 shorter events, 271.7 us)
Async XLA Ops:
  7.2 6.6 copy-start.23
  7.2 53.0 %all-gather.10.cloned.1.call-start = ((), (), s32[]{:S(2)}) async-start(), calls=%async_computation.9 | async-start | bytes 1769472 | tf_op jit(solution)/shard_map/all_gather | solution.py:148
  7.9 87.5 %all-gather.8.cloned.1.call-start = ((), (), s32[]{:S(2)}) async-start(), calls=%async_computation.8 | async-start | bytes 5242880 | tf_op jit(solution)/shard_map/all_gather | solution.py:157
  13.7 223.2 %reduce-scatter.15.cloned.1.call-start = ((), (), s32[]{:S(2)}) async-start(), calls=%async_computation.10 | async-start | bytes 10485760 | tf_op jit(solution)/shard_map/reduce_scatter | solution.py:169
  156.6 8.7 copy-start.1
  156.6 8.7 copy-start.4
  165.3 74.1 %copy-start.26 = (f32[1024]{0:T(1024)S(1)}, f32[1024]{0:T(1024)}, u32[]{:S(2)}) copy-start(f32[1024]{0:T(1024)} %param.17) | copy-start | bytes 12292
  165.3 130.7 %all-gather.14.cloned.1.call-start = ((), (), s32[]{:S(2)}) async-start(), calls=%async_computation.12 | async-start | bytes 3022848 | tf_op jit(solution)/shard_map/all_gather | solution.py:150
  165.9 164.7 %all-gather.12.cloned.1.call-start = ((), (), s32[]{:S(2)}) async-start(), calls=%async_computation.11 | async-start | bytes 5242880 | tf_op jit(solution)/shard_map/all_gather | solution.py:179
  240.7 133.8 %all-gather.16.cloned.1.call-start = ((), (), s32[]{:S(2)}) async-start(), calls=%async_computation.13 | async-start | bytes 1511424 | tf_op jit(solution)/shard_map/all_gather | solution.py:151
  241.3 211.9 %reduce-scatter.17.cloned.1.call-start = ((), (), s32[]{:S(2)}) async-start(), calls=%async_computation.14 | async-start | bytes 10485760 | tf_op jit(solution)/shard_map/reduce_scatter | solution.py:187
  383.4 108.6 %all-gather.18.cloned.1.call-start = ((), (), s32[]{:S(2)}) async-start(), calls=%async_computation.15 | async-start | bytes 5242880 | tf_op jit(solution)/shard_map/all_gather | solution.py:198
  457.4 128.0 %reduce-scatter.19.cloned.1.call-start = ((), (), s32[]{:S(2)}) async-start(), calls=%async_computation.16 | async-start | bytes 10485760 | tf_op jit(solution)/shard_map/reduce_scatter | solution.py:211
  492.0 12.9 %copy-start.31 = (bf16[2,656,1024]{2,1,0:T(8,128)(2,1)S(1)}, bf16[2,656,1024]{2,1,0:T(8,128)(2,1)}, u32[]{:S(2)}) copy-start(bf16[2,656,1024]{2,1,0:T(8,128)(2,1)} %all-gather.14.cloned.1.call-done) | copy-start | bytes 8060932
  513.9 115.0 %all-gather.20.cloned.1.call-start = ((), (), s32[]{:S(2)}) async-start(), calls=%async_computation.17 | async-start | bytes 5242880 | tf_op jit(solution)/shard_map/all_gather | solution.py:220
  585.5 4.7 copy-start.7
  585.5 4.7 copy-start.9
  593.6 250.1 %reduce-scatter.29.cloned.1.call-start = ((), (), s32[]{:S(2)}) async-start(), calls=%async_computation.22 | async-start | bytes 1769472
  601.2 244.5 %reduce-scatter.27.cloned.1.call-start = ((), (), s32[]{:S(2)}) async-start(), calls=%async_computation.21 | async-start | bytes 3244032
  620.8 8.2 copy-start.19
  628.4 6.6 copy-start.2
  628.4 246.6 %reduce-scatter.23.cloned.1.call-start = ((), (), s32[]{:S(2)}) async-start(), calls=%async_computation.19 | async-start | bytes 589824 | tf_op jit(solution)/shard_map/reduce_scatter | solution.py:262
  802.3 4.8 copy-start.5
  802.3 4.8 copy-start.13
  812.2 130.6 %reduce-scatter.25.cloned.1.call-start = ((), (), s32[]{:S(2)}) async-start(), calls=%async_computation.20 | async-start | bytes 1769472
  835.3 153.3 %reduce-scatter.21.cloned.1.call-start = ((), (), s32[]{:S(2)}) async-start(), calls=%async_computation.18 | async-start | bytes 5242880 | tf_op jit(solution)/shard_map/reduce_scatter | solution.py:236
  842.8 145.8 %copy-start.3 = (bf16[512,1024]{1,0:T(8,128)(2,1)S(1)}, bf16[512,1024]{1,0:T(8,128)(2,1)}, u32[]{:S(2)}) copy-start(bf16[512,1024]{1,0:T(8,128)(2,1)} %param.13) | copy-start | bytes 3145732
  842.8 145.8 %copy-start.25 = (f32[512]{0:T(512)S(1)}, f32[512]{0:T(512)}, u32[]{:S(2)}) copy-start(f32[512]{0:T(512)} %copy-done.24) | copy-start | bytes 6148
  842.8 145.8 %copy-start.27 = (f32[1024]{0:T(1024)S(1)}, f32[1024]{0:T(1024)}, u32[]{:S(2)}) copy-start(f32[1024]{0:T(1024)} %param.16) | copy-start | bytes 12292
  842.8 145.8 %copy-start.29 = (f32[512]{0:T(512)S(1)}, f32[512]{0:T(512)}, u32[]{:S(2)}) copy-start(f32[512]{0:T(512)} %copy-done.28) | copy-start | bytes 6148
  842.9 148.0 %copy-start.30 = (f32[1024]{0:T(1024)S(1)}, f32[1024]{0:T(1024)}, u32[]{:S(2)}) copy-start(f32[1024]{0:T(1024)} %get-tuple-element.261) | copy-start | bytes 12292
  842.9 188.4 %copy-start.10 = (f32[512,1024]{1,0:T(8,128)S(1)}, f32[512,1024]{1,0:T(8,128)}, u32[]{:S(2)}) copy-start(f32[512,1024]{1,0:T(8,128)} %get-tuple-element.308) | copy-start | bytes 6291460
  (21 other events, 57.0 us)
Sparse Core Ops, SparseCore 0:
  10.0 50.0 all-gather.9
  62.3 33.0 all-gather.7
  165.4 71.4 reduce-scatter.14
  238.8 57.1 all-gather.13
  298.0 32.6 all-gather.11
  332.5 41.9 all-gather.15
  383.6 69.5 reduce-scatter.16
  457.6 34.4 all-gather.17
  514.0 71.3 reduce-scatter.18
  593.7 34.4 all-gather.19
  631.6 65.7 reduce-scatter.28
  700.9 71.3 reduce-scatter.26
  812.4 62.5 reduce-scatter.22
  878.2 64.6 reduce-scatter.24
  945.2 43.3 reduce-scatter.20
where the time goes:
time: 1050 us; the launch traced here: 1040 us
  waiting for transfers between devices  529 us (50%)
  matrix products  241 us (23%)
  other arithmetic  112 us (11%)
  blocking collectives  76.3 us (7%)
  local copies, waits for them, and re-layouts  62.1 us (6%)
  between operations  17.3 us (2%)
    reduce_scatter x1, waiting for transfers between devices, shards(): lax.psum_scatter(jnp.einsum('rif,ifd->rd', part, feed_in_rows, preferred_...  71.5 us
    reduce_scatter x1, waiting for transfers between devices, shards(): lax.psum_scatter(jnp.einsum('rc,oc->ro', part, attention_rows, preferred_...  70.8 us
    unnamed x18, waiting for transfers between devices  68.4 us
    reduce_scatter x1, waiting for transfers between devices, shards(): lax.psum_scatter(jnp.einsum('rf,of->ro', part, feed_out_rows, preferred_e...  68.3 us
    all_gather x1, waiting for transfers between devices, shards(): lax.all_gather(feed_in, 'row', axis=2, tiled=True)  54.6 us
    reduce_scatter x1, waiting for transfers between devices, shards(): lax.psum_scatter(jnp.einsum('ric,icd->rd', part, joint_rows, preferred_el...  42.2 us
    psum x1, blocking collectives, shards(): totals = lax.psum((grad_first, grad_second, squares), ('row', 'col'))  39.7 us
    unnamed x77, local copies, waits for them, and re-layouts  38.5 us
  transfers between devices with their start and end apart: 15, of which 12 were waited for; matrix products, arithmetic and copies ran while one was open for 27% of the time, Pallas kernels for 0%

commit v1 on v0

--- a/solution.py
+++ b/solution.py
@@ -1,7 +1,9 @@
+import functools
 import jax
 import jax.numpy as jnp
 from jax import lax
 from jax.sharding import PartitionSpec as P
+from jax.lax import axis_index, axis_size, ppermute
 
 D = 1024
 HD = 64
@@ -9,6 +11,39 @@
 EPSILON = 1e-05
 ROPE_BASE = 160000.0
 FLOOR_SCORE = -1e30
+
+
+def leaves_treat(payload, axis_no):
+    t_next = list(payload.shape[1:])
+    t_next[axis_no] *= payload.shape[0]
+    aux = jnp.moveaxis(payload, 0, axis_no).reshape(t_next)
+    return aux
+
+
+def touch_the_corner(patch, mesh_dim, dim_i):
+    axis_n = axis_size(mesh_dim)
+    everything = range(axis_n)
+    piece_now = map(lambda d: (d, (d + 1) % axis_n), everything)
+    pool = list(piece_now)
+    table = [(w, dev) for dev, w in pool]
+    b_now, block_now = ([], [])
+    for no in range(axis_n - 1):
+        if no % 2 == 0:
+            parts_out = ppermute(b_now[-1] if b_now else patch, axis_name=mesh_dim, perm=pool)
+            b_now.append(parts_out)
+        else:
+            latest = ppermute(block_now[-1] if block_now else patch, axis_name=mesh_dim, perm=table)
+            block_now.append(latest)
+    opened = jnp.stack([*b_now[::-1], patch, *block_now], axis=0)
+    r1 = axis_index(mesh_dim)
+    step_out = len(b_now)
+    y = r1 - step_out
+    opened = opened[(jnp.arange(axis_n) - y) % axis_n]
+    tile_out = leaves_treat(opened, dim_i)
+    return tile_out
+
+
+follow_sums_all_on = functools.partial(touch_the_corner, mesh_dim="row", dim_i=2)
 
 
 def layer_norm(values, gain):
@@ -147,7 +182,7 @@
     joint_rows, attention_rows, feed_in_rows, feed_out_rows = (
         lax.all_gather(attention_in, "row", axis=2, tiled=True),
         lax.all_gather(attention_out, "row", axis=0, tiled=True),
-        lax.all_gather(feed_in, "row", axis=2, tiled=True),
+        follow_sums_all_on(feed_in),
         lax.all_gather(feed_out, "row", axis=0, tiled=True),
     )
     inputs = hidden_in.astype(jnp.float32)

time: 1050 us -> 1020 us (0.971)
  waiting for transfers between devices: 529 us -> 451 us
  starting transfers between devices: 1.47 us -> 31.1 us
  local copies, waits for them, and re-layouts: 62.1 us -> 78.9 us
    all_gather x1 -> x0, waiting for transfers between devices: 54.6 us -> none  [shards(): lax.all_gather(feed_in, 'row', axis=2, tiled=True)]
    all_gather x1, waiting for transfers between devices: 34.6 us -> 0.01 us  [shards(): lax.all_gather(low_two, 'col', axis=0, tiled=True)]
    ppermute x0 -> x7, starting transfers between devices: none -> 29.6 us  [the longest x3 23.1 us: touch_the_corner(): ppermute(block_now[-1] if block_now else patch, axis_name=mesh_dim, perm=...]
    ppermute x0 -> x7, waiting for transfers between devices: none -> 29 us  [the longest x4 29 us: touch_the_corner(): ppermute(b_now[-1] if b_now else patch, axis_name=mesh_dim, perm=pool)]
    all_gather x1, waiting for transfers between devices: 18.4 us -> 0.01 us  [shards(): lax.all_gather(feed_out, 'row', axis=0, tiled=True)]
    unnamed x77 -> x92, local copies, waits for them, and re-layouts: 38.5 us -> 50.3 us
    unnamed x18 -> x17, waiting for transfers between devices: 68.4 us -> 67.4 us
  transfers between devices with their start and end apart: 15 -> 21, of which waited for: 12 -> 13; matrix products, arithmetic and copies ran while one was open for 27% -> 29% of each run, Pallas kernels for 0% -> 0%
where the time goes in v1:
time: 1020 us; the launch traced here: 1010 us
  waiting for transfers between devices  451 us (44%)
  matrix products  241 us (24%)
  other arithmetic  112 us (11%)
  local copies, waits for them, and re-layouts  78.9 us (8%)
  blocking collectives  76.3 us (7%)
  starting transfers between devices  31.1 us (3%)
  between operations  17.3 us (2%)
    reduce_scatter x1, waiting for transfers between devices, shards(): lax.psum_scatter(jnp.einsum('rif,ifd->rd', part, feed_in_rows, preferred_...  71.5 us
    reduce_scatter x1, waiting for transfers between devices, shards(): lax.psum_scatter(jnp.einsum('rc,oc->ro', part, attention_rows, preferred_...  71.3 us
    reduce_scatter x1, waiting for transfers between devices, shards(): lax.psum_scatter(jnp.einsum('rf,of->ro', part, feed_out_rows, preferred_e...  69.1 us
    unnamed x17, waiting for transfers between devices  67.4 us
    unnamed x92, local copies, waits for them, and re-layouts  50.3 us
    reduce_scatter x1, waiting for transfers between devices, shards(): lax.psum_scatter(jnp.einsum('ric,icd->rd', part, joint_rows, preferred_el...  42.2 us
    psum x1, blocking collectives, shards(): totals = lax.psum((grad_first, grad_second, squares), ('row', 'col'))  39.7 us
    dot_general x4, matrix products, one_block(): jnp.einsum('qhd,khd->hqk', grad_block, seq_values, preferred_element_type...  37.7 us
  transfers between devices with their start and end apart: 21, of which 13 were waited for; matrix products, arithmetic and copies ran while one was open for 29% of the time, Pallas kernels for 0%

profile of v1, /device:TPU:0, one launch (start us, length us, event | category | flops | bytes accessed | tf_op | source)
XLA Modules:
  0.0 1010.6 jit_solution(4973920490419649821)
XLA Ops:
  13.8 36.7 %all_gather.25 = bf16[1024,256]{1,0:T(8,128)(2,1)} all-gather(bf16[128,256]{1,0:T(8,128)(2,1)S(1)} %copy-done.28), channel_id=1, replica_groups=mesh['row'=8,'col'=4] {'row'}, dimensions={0}, use_global_device_ids=true | all-gather | bytes 589824 | tf_op jit(solution)/shard_map/all_gather | solution.py:184
  60.2 35.2 %all-gather.7.cloned.1.call-done = bf16[2048,1024]{1,0:T(8,128)(2,1)} async-done(((bf16[512,1024]{1,0:T(8,128)(2,1)}), bf16[2048,1024]{1,0:T(8,128)(2,1)}) %all-gather.7.cloned.1.call-update) | async-done | bytes 4194320 | tf_op jit(solution)/shard_map/all_gather | solution.py:192
  104.2 52.4 %while.30 = (s32[]{:T(128)}, bf16[4,512,4,64]{1,3,2,0:T(8,128)(2,1)}, f32[4,4,512]{2,1,0:T(4,128)S(1)}, s32[2048]{0:T(1024)S(1)}, s32[4]{0:T(128)S(1)}, /*index=...) while((s32[]{:T(128)}, ...), condition=%wide.region_5.6_spmd, body=%wide.region_2.0_spmd.sunk | while | flops 1124204544 | bytes 53035200 | solution.py:111
  165.6 71.3 %reduce-scatter.15.cloned.1.call-done = f32[512,1024]{1,0:T(8,128)} async-done(((f32[2048,1024]{1,0:T(8,128)}), f32[512,1024]{1,0:T(8,128)}) %reduce-scatter.15.cloned.1.call-update) | async-done | bytes 2097168 | tf_op jit(solution)/shard_map/reduce_scatter | solution.py:204
  242.4 10.7 %collective-permute-done = bf16[2,656,128]{2,1,0:T(8,128)(2,1)S(1)} collective-permute-done((bf16[2,656,128]{2,1,0:T(8,128)(2,1)S(1)}, bf16[2,656,128]{2,1,0:T(8,128)(2,1)S(1)}, u32[]{:S(2)}, u32[]{:S(2)}) %collective-permute-start) | collective-permute-done | bytes 335904 | tf_op jit(solution)/shard_map/ppermute | solution.py:32
  257.8 8.9 collective-permute-done.1
  269.1 8.4 collective-permute-start.5
  284.9 10.0 collective-permute-start.6
  315.7 8.5 fusion.59
  328.3 12.9 %multiply_convert_fusion.2 = (bf16[2048,656]{0,1:T(8,128)(2,1)}, f32[2048,656]{0,1:T(8,128)}) fusion(f32[2048,2,656]{0,2,1:T(8,128)S(1)} %fusion.59), kind=kLoop, calls=%fused_computation.64 | loop fusion | flops 88670208 | bytes 18808832 | tf_op jit(solution)/shard_map/convert_element_type | solution.py:220
  341.2 9.0 fusion.117
  351.7 69.1 %reduce-scatter.17.cloned.1.call-done = f32[512,1024]{1,0:T(8,128)} async-done(((f32[2048,1024]{1,0:T(8,128)}), f32[512,1024]{1,0:T(8,128)}) %reduce-scatter.17.cloned.1.call-update) | async-done | bytes 2097168 | tf_op jit(solution)/shard_map/reduce_scatter | solution.py:222
  425.3 34.3 %all-gather.15.cloned.1.call-done = bf16[2048,1024]{1,0:T(8,128)(2,1)} async-done(((bf16[512,1024]{1,0:T(8,128)(2,1)}), bf16[2048,1024]{1,0:T(8,128)(2,1)}) %all-gather.15.cloned.1.call-update) | async-done | bytes 4194320 | tf_op jit(solution)/shard_map/all_gather | solution.py:233
  459.6 10.4 %fusion.68 = (bf16[2048,1,656]{0,2,1:T(8,128)(2,1)S(1)}, bf16[2048,1,656]{0,2,1:T(8,128)(2,1)S(1)}) fusion(f32[2048,656]{0,1:T(8,128)} %get-tuple-element.310, f32[2048,2,656]{0,2,1:T(8,128)} %copy-done.9, bf16[2048,1024]{1,0:T(8,128)(2,1)} %all-gather.15.cloned.1.call-done, bf16[1024,656]{0,1:T(8,128)(2,1)} %all-gather.13.cloned.1.call-done), kind=kOutput, calls=%fused_computation.95 | convolution fusion | flops 2775646208 | bytes 27033600 | tf_op jit(solution)/shard_map/ro,of->rf/dot_general | solution.py:236
  472.4 9.0 convolution_bitcast_fusion
  481.5 71.5 %reduce-scatter.19.cloned.1.call-done = f32[512,1024]{1,0:T(8,128)} async-done(((f32[2048,1024]{1,0:T(8,128)}), f32[512,1024]{1,0:T(8,128)}) %reduce-scatter.19.cloned.1.call-update) | async-done | bytes 2097168 | tf_op jit(solution)/shard_map/reduce_scatter | solution.py:246
  568.8 10.8 %fusion.78 = bf16[2,656,1024]{2,1,0:T(8,128)(2,1)} fusion(bf16[2048,1024]{1,0:T(8,128)(2,1)} %all-gather.11.cloned.1.call-done, bf16[2048,1,656]{0,2,1:T(8,128)(2,1)} %copy-done.37, bf16[2048,1,656]{0,2,1:T(8,128)(2,1)} %copy-done.36), kind=kOutput, calls=%fused_computation.108 | convolution fusion | flops 5506957312 | bytes 12255232 | tf_op jit(solution)/shard_map/rif,rd->ifd/dot_general | solution.py:287
  579.6 8.7 copy.37
  588.2 7.5 reshape.256
  602.8 167.4 %while.31 = (s32[]{:T(128)}, f32[2048,4,64]{0,2,1:T(8,128)}, f32[2048,4,64]{0,2,1:T(8,128)}, f32[2048,4,64]{0,2,1:T(8,128)}, s32[2048]{0:T(1024)S(1)}, /*index=5...) while((s32[]{:T(128)}, f32[2048,4,64]{0,2,1:T(8,128)}, ...), condition=%wide.region_19.20_spmd.clone, body=%wide.region_17.19_spmd.clone.sunk | while | flops 2750021632 | bytes 172564736 | solution.py:159
  612.0 9.5 multiply_reduce_fusion.8
  621.4 8.2 multiply_convert_fusion.5
  653.4 9.4 multiply_reduce_fusion.8
  662.8 8.2 multiply_convert_fusion.5
  695.4 9.5 multiply_reduce_fusion.8
  704.9 8.2 multiply_convert_fusion.5
  737.7 9.4 multiply_reduce_fusion.8
  747.1 8.1 multiply_convert_fusion.5
  819.4 23.7 %reduce-scatter.23.cloned.1.call-done = bf16[128,256]{1,0:T(8,128)(2,1)} async-done(((bf16[1024,256]{1,0:T(8,128)(2,1)}), bf16[128,256]{1,0:T(8,128)(2,1)}) %reduce-scatter.23.cloned.1.call-update) | async-done | bytes 65552 | tf_op jit(solution)/shard_map/reduce_scatter | solution.py:297
  844.6 66.5 %reduce-scatter.25.cloned.1.call-done = bf16[128,768]{1,0:T(8,128)(2,1)} async-done(((bf16[1024,768]{1,0:T(8,128)(2,1)}), bf16[128,768]{1,0:T(8,128)(2,1)}) %reduce-scatter.25.cloned.1.call-update) | async-done | bytes 196624
  914.6 42.2 %reduce-scatter.21.cloned.1.call-done = bf16[512,1024]{1,0:T(8,128)(2,1)} async-done(((bf16[2048,1024]{1,0:T(8,128)(2,1)}), bf16[512,1024]{1,0:T(8,128)(2,1)}) %reduce-scatter.21.cloned.1.call-update) | async-done | bytes 1048592 | tf_op jit(solution)/shard_map/reduce_scatter | solution.py:271
  959.1 39.7 %all-reduce = (f32[]{:T(128)}, f32[1024]{0:T(1024)}, f32[1024]{0:T(1024)}) all-reduce(f32[]{:T(128)} %multiply_reduce_fusion.6, f32[1024]{0:T(1024)S(1)} %get-tuple-element.264, f32[1024]{0:T(1024)S(1)} %copy-done.35), channel_id=1, replica_groups=mesh['row'=8,'col'=4] {'row','col'}, use_global_device_ids=true, to_apply=%region_12.13 | all-reduce | flops 2049 | bytes 16392 | tf_op jit(solution)/shard_map/psum | solution.py:307
  (252 shorter events, 315.2 us)
Async XLA Ops:
  7.2 53.0 %all-gather.9.cloned.1.call-start = ((), (), s32[]{:S(2)}) async-start(), calls=%async_computation.9 | async-start | bytes 1769472 | tf_op jit(solution)/shard_map/all_gather | solution.py:183
  7.9 87.5 %all-gather.7.cloned.1.call-start = ((), (), s32[]{:S(2)}) async-start(), calls=%async_computation.8 | async-start | bytes 5242880 | tf_op jit(solution)/shard_map/all_gather | solution.py:192
  13.7 223.2 %reduce-scatter.15.cloned.1.call-start = ((), (), s32[]{:S(2)}) async-start(), calls=%async_computation.10 | async-start | bytes 10485760 | tf_op jit(solution)/shard_map/reduce_scatter | solution.py:204
  156.6 8.7 copy-start.1
  165.4 74.1 %copy-start.31 = (f32[1024]{0:T(1024)S(1)}, f32[1024]{0:T(1024)}, u32[]{:S(2)}) copy-start(f32[1024]{0:T(1024)} %param.17) | copy-start | bytes 12292
  165.4 150.3 %all-gather.11.cloned.1.call-start = ((), (), s32[]{:S(2)}) async-start(), calls=%async_computation.11 | async-start | bytes 5242880 | tf_op jit(solution)/shard_map/all_gather | solution.py:214
  240.8 100.4 %all-gather.13.cloned.1.call-start = ((), (), s32[]{:S(2)}) async-start(), calls=%async_computation.12 | async-start | bytes 1511424 | tf_op jit(solution)/shard_map/all_gather | solution.py:186
  240.9 12.2 %collective-permute-start = (bf16[2,656,128]{2,1,0:T(8,128)(2,1)S(1)}, bf16[2,656,128]{2,1,0:T(8,128)(2,1)S(1)}, u32[]{:S(2)}, u32[]{:S(2)}) collective-permute-start(bf16[2,656,128]{2,1,0:T(8,128)(2,1)S(1)} %copy-done.25), channel_id=1, source_target_pairs={{0,4},{4,8},{8,12},{12,16},{16,20},{20,24},{24,28},{28,0},{1,5},{5... | collective-permute-start | bytes 1007624 | tf_op jit(solution)/shard_map/ppermute | solution.py:32
  253.0 16.1 %copy-start.26 = (bf16[2,656,128]{2,1,0:T(8,128)(2,1)}, bf16[2,656,128]{2,1,0:T(8,128)(2,1)S(1)}, u32[]{:S(2)}) copy-start(bf16[2,656,128]{2,1,0:T(8,128)(2,1)S(1)} %collective-permute-done) | copy-start | bytes 1007620
  253.0 13.6 %collective-permute-start.1 = (bf16[2,656,128]{2,1,0:T(8,128)(2,1)S(1)}, bf16[2,656,128]{2,1,0:T(8,128)(2,1)S(1)}, u32[]{:S(2)}, u32[]{:S(2)}) collective-permute-start(bf16[2,656,128]{2,1,0:T(8,128)(2,1)S(1)} %collective-permute-done), channel_id=1, source_target_pairs={{0,4},{4,8},{8,12},{12,16},{16,20},{20,24},{24,28},{28,0},{1,5},{5... | collective-permute-start | bytes 1007624 | tf_op jit(solution)/shard_map/ppermute | solution.py:32
  253.0 16.1 %collective-permute-start.4 = (bf16[2,656,128]{2,1,0:T(8,128)(2,1)S(1)}, bf16[2,656,128]{2,1,0:T(8,128)(2,1)}, u32[]{:S(2)}, u32[]{:S(2)}) collective-permute-start(bf16[2,656,128]{2,1,0:T(8,128)(2,1)S(1)} %copy-done.25), channel_id=1, source_target_pairs={{4,0},{8,4},{12,8},{16,12},{20,16},{24,20},{28,24},{0,28},{5,1},{9... | collective-permute-start | bytes 1007624 | tf_op jit(solution)/shard_map/ppermute | solution.py:35
  266.6 10.9 %copy-start.27 = (bf16[2,656,128]{2,1,0:T(8,128)(2,1)}, bf16[2,656,128]{2,1,0:T(8,128)(2,1)S(1)}, u32[]{:S(2)}) copy-start(bf16[2,656,128]{2,1,0:T(8,128)(2,1)S(1)} %collective-permute-done.1) | copy-start | bytes 1007620
  266.6 15.6 %collective-permute-start.2 = (bf16[2,656,128]{2,1,0:T(8,128)(2,1)S(1)}, bf16[2,656,128]{2,1,0:T(8,128)(2,1)}, u32[]{:S(2)}, u32[]{:S(2)}) collective-permute-start(bf16[2,656,128]{2,1,0:T(8,128)(2,1)S(1)} %collective-permute-done.1), channel_id=1, source_target_pairs={{0,4},{4,8},{8,12},{12,16},{16,20},{20,24},{24,28},{28,0},{1,5},{5... | collective-permute-start | bytes 1007624 | tf_op jit(solution)/shard_map/ppermute | solution.py:32
  269.1 15.8 %collective-permute-start.5 = (bf16[2,656,128]{2,1,0:T(8,128)(2,1)}, bf16[2,656,128]{2,1,0:T(8,128)(2,1)}, u32[]{:S(2)}, u32[]{:S(2)}) collective-permute-start(bf16[2,656,128]{2,1,0:T(8,128)(2,1)} %collective-permute-done.4), channel_id=1, source_target_pairs={{4,0},{8,4},{12,8},{16,12},{20,16},{24,20},{28,24},{0,28},{5,1},{9... | collective-permute-start | bytes 1007624 | tf_op jit(solution)/shard_map/ppermute | solution.py:35
  282.2 17.4 %collective-permute-start.3 = (bf16[2,656,128]{2,1,0:T(8,128)(2,1)}, bf16[2,656,128]{2,1,0:T(8,128)(2,1)}, u32[]{:S(2)}, u32[]{:S(2)}) collective-permute-start(bf16[2,656,128]{2,1,0:T(8,128)(2,1)} %collective-permute-done.2), channel_id=1, source_target_pairs={{0,4},{4,8},{8,12},{12,16},{16,20},{20,24},{24,28},{28,0},{1,5},{5... | collective-permute-start | bytes 1007624 | tf_op jit(solution)/shard_map/ppermute | solution.py:32
  284.8 136.0 %reduce-scatter.17.cloned.1.call-start = ((), (), s32[]{:S(2)}) async-start(), calls=%async_computation.13 | async-start | bytes 10485760 | tf_op jit(solution)/shard_map/reduce_scatter | solution.py:222
  284.9 25.9 %collective-permute-start.6 = (bf16[2,656,128]{2,1,0:T(8,128)(2,1)}, bf16[2,656,128]{2,1,0:T(8,128)(2,1)S(1)}, u32[]{:S(2)}, u32[]{:S(2)}) collective-permute-start(bf16[2,656,128]{2,1,0:T(8,128)(2,1)} %collective-permute-done.5), channel_id=1, source_target_pairs={{4,0},{8,4},{12,8},{16,12},{20,16},{24,20},{28,24},{0,28},{5,1},{9... | collective-permute-start | bytes 1007624 | tf_op jit(solution)/shard_map/ppermute | solution.py:35
  350.2 109.5 %all-gather.15.cloned.1.call-start = ((), (), s32[]{:S(2)}) async-start(), calls=%async_computation.14 | async-start | bytes 5242880 | tf_op jit(solution)/shard_map/all_gather | solution.py:233
  425.0 128.0 %reduce-scatter.19.cloned.1.call-start = ((), (), s32[]{:S(2)}) async-start(), calls=%async_computation.15 | async-start | bytes 10485760 | tf_op jit(solution)/shard_map/reduce_scatter | solution.py:246
  459.6 12.8 %copy-start.19 = (bf16[8,2,656,128]{3,2,1,0:T(8,128)(2,1)S(1)}, bf16[8,2,656,128]{3,2,1,0:T(8,128)(2,1)}, u32[]{:S(2)}) copy-start(bf16[8,2,656,128]{3,2,1,0:T(8,128)(2,1)} %gather_fusion) | copy-start | bytes 8060932
  481.5 114.8 %all-gather.17.cloned.1.call-start = ((), (), s32[]{:S(2)}) async-start(), calls=%async_computation.16 | async-start | bytes 5242880 | tf_op jit(solution)/shard_map/all_gather | solution.py:255
  561.1 250.4 %reduce-scatter.29.cloned.1.call-start = ((), (), s32[]{:S(2)}) async-start(), calls=%async_computation.21 | async-start | bytes 1769472
  568.7 244.6 %reduce-scatter.27.cloned.1.call-start = ((), (), s32[]{:S(2)}) async-start(), calls=%async_computation.20 | async-start | bytes 3244032
  595.8 247.3 %reduce-scatter.23.cloned.1.call-start = ((), (), s32[]{:S(2)}) async-start(), calls=%async_computation.18 | async-start | bytes 589824 | tf_op jit(solution)/shard_map/reduce_scatter | solution.py:297
  780.2 130.9 %reduce-scatter.25.cloned.1.call-start = ((), (), s32[]{:S(2)}) async-start(), calls=%async_computation.19 | async-start | bytes 1769472
  803.2 153.7 %reduce-scatter.21.cloned.1.call-start = ((), (), s32[]{:S(2)}) async-start(), calls=%async_computation.17 | async-start | bytes 5242880 | tf_op jit(solution)/shard_map/reduce_scatter | solution.py:271
  810.7 146.2 %copy-start.4 = (bf16[512,1024]{1,0:T(8,128)(2,1)S(1)}, bf16[512,1024]{1,0:T(8,128)(2,1)}, u32[]{:S(2)}) copy-start(bf16[512,1024]{1,0:T(8,128)(2,1)} %param.13) | copy-start | bytes 3145732
  810.7 146.1 %copy-start.30 = (f32[512]{0:T(512)S(1)}, f32[512]{0:T(512)}, u32[]{:S(2)}) copy-start(f32[512]{0:T(512)} %copy-done.29) | copy-start | bytes 6148
  810.7 146.1 %copy-start.32 = (f32[1024]{0:T(1024)S(1)}, f32[1024]{0:T(1024)}, u32[]{:S(2)}) copy-start(f32[1024]{0:T(1024)} %param.16) | copy-start | bytes 12292
  810.7 146.1 %copy-start.34 = (f32[512]{0:T(512)S(1)}, f32[512]{0:T(512)}, u32[]{:S(2)}) copy-start(f32[512]{0:T(512)} %copy-done.33) | copy-start | bytes 6148
  814.8 144.3 %copy-start.35 = (f32[1024]{0:T(1024)S(1)}, f32[1024]{0:T(1024)}, u32[]{:S(2)}) copy-start(f32[1024]{0:T(1024)} %get-tuple-element.261) | copy-start | bytes 12292
  814.8 184.6 %copy-start.11 = (f32[512,1024]{1,0:T(8,128)S(1)}, f32[512,1024]{1,0:T(8,128)}, u32[]{:S(2)}) copy-start(f32[512,1024]{1,0:T(8,128)} %get-tuple-element.308) | copy-start | bytes 6291460
  (31 other events, 96.8 us)
Sparse Core Ops, SparseCore 0:
  10.0 50.0 all-gather.8
  62.3 33.0 all-gather.6
  165.5 71.4 reduce-scatter.14
  240.9 34.4 all-gather.10
  284.9 43.1 all-gather.12
  350.3 70.4 reduce-scatter.16
  425.2 34.4 all-gather.14
  481.6 71.4 reduce-scatter.18
  561.2 34.4 all-gather.16
  599.0 65.7 reduce-scatter.28
  668.4 71.0 reduce-scatter.26
  780.3 62.7 reduce-scatter.22
  846.5 64.5 reduce-scatter.24
  913.5 43.3 reduce-scatter.20
